TPU v7x, 256 devices: a whole 4x4x8 slice. The times are simulated.
256 devices in a mesh: slot: 8 (over y_lo, x), feat: 32 (over y_hi, z, core).
Axes of the slice: x: 4, y: 4 (y_hi: 2, y_lo: 2; y = y_hi * 2 + y_lo), z: 8, core: 2. Of those that a mesh axis runs over, the one named last changes fastest.
Arguments:
- acts_in: bfloat16 [3, 256, 2304], P(None, None, 'slot'), may hold values from -6 to 6
- acts_out: bfloat16 [3, 256, 2304], P(None, None, 'slot'), may hold values from -6 to 6
- enc_weight: bfloat16 [3, 2304, 16384], P(None, 'slot', 'feat'), may hold values from -0.125 to 0.125
- enc_bias: float32 [3, 16384], P(None, 'feat'), may hold values from -3 to 3
- dec_weight: bfloat16 [6, 16384, 2304], P(None, 'feat', 'slot'), may hold values from -0.046875 to 0.046875
- dec_bias: float32 [3, 2304], P(None, 'slot'), may hold values from -3 to 3
Outputs:
- enc_grad: float32 [3, 2304, 16384], P(None, 'slot', 'feat')
- enc_bias_grad: float32 [3, 16384], P(None, 'feat')
- dec_grad: float32 [6, 16384, 2304], P(None, 'feat', 'slot')
- mse: float32 [], replicated
All inputs are finite; a program needn't handle non-finite values.
Results may differ from a plain program's by a relative error of at most 0.0095.
Values may be sent and summed in bfloat16 or wider, within the bound.
No kernel may reach another device: no remote copies, remote signals or barrier semaphores. Data moves between devices by JAX's collectives and lax.ppermute only.
A program may use at most 64 MiB of HBM per device.

v0:
```python
import functools
import jax
import jax.numpy as jnp
from jax import lax
from jax.sharding import Mesh
from jax.sharding import PartitionSpec as P

D = 2304
SLOT = ("slot_0", "slot_1")
FEAT = ("feat_0", "feat_1", "feat_2")
SLOT_FEAT = ("slot_0", "slot_1", "feat_0", "feat_1", "feat_2")


def cut_along(x, dim, devices):
    before, after = (x.shape[:dim], x.shape[dim + 1 :])
    return jnp.moveaxis(x.reshape(*before, devices, -1, *after), dim, 0)


def sum_at_owner(x, axis, dim):
    tiles = cut_along(x, dim, lax.axis_size(axis))
    arrived = lax.all_to_all(tiles, axis, split_axis=0, concat_axis=0, tiled=True)
    return arrived.sum(axis=0)


def over_axes(x, axes):
    return functools.reduce(lax.psum, axes, x)


def sent_to_all(x, axis):
    devices = lax.axis_size(axis)
    return lax.all_to_all(jnp.broadcast_to(x[None], (devices, *x.shape)), axis, 0, 0, tiled=True)


def joined_along(tiles, dim):
    dims = list(tiles.shape[1:])
    dims[dim] *= tiles.shape[0]
    return jnp.moveaxis(tiles, 0, dim).reshape(dims)


def collect(x, axis, dim):
    tiles = sent_to_all(x, axis)
    return joined_along(tiles, dim)


def activate(preact):
    return (
        jnp.maximum(preact, 0.0).astype(jnp.bfloat16),
        jnp.where(preact > 0, 1.0, 0.0).astype(jnp.bfloat16),
    )


def local(acts_in, acts_out, enc_weight, enc_bias, dec_weight, dec_bias):
    layers = acts_in.shape[0]
    tokens = acts_in.shape[1]
    width_dev = acts_in.shape[2]
    feature_dev = enc_weight.shape[2]
    pair_list = [(a, b) for a in range(layers) for b in range(a, layers)]

    def encode_rows():
        pieces = [
            jnp.dot(acts_in[a], enc_weight[a], preferred_element_type=jnp.float32)
            for a in range(layers)
        ]
        return jnp.concatenate(pieces, axis=1)

    bias_row = enc_bias.reshape(1, layers * feature_dev)
    preact = lax.psum(encode_rows(), SLOT) + bias_row
    features, slopes = activate(preact)
    target = (
        jnp.transpose(acts_out, (1, 0, 2)).reshape(tokens, layers * width_dev).astype(jnp.float32)
    )
    dec_row = dec_bias.reshape(1, layers * width_dev)
    portion = tokens // lax.axis_size(FEAT)
    row_block = features
    pieces = []
    for decode_b in range(layers):
        summed = jnp.zeros((portion * lax.axis_size(FEAT), width_dev), jnp.float32)
        for decode_a in range(decode_b + 1):
            pair_num = pair_list.index((decode_a, decode_b))
            summed = summed + jnp.dot(
                row_block[:, decode_a * feature_dev : (decode_a + 1) * feature_dev],
                dec_weight[pair_num],
                preferred_element_type=jnp.float32,
            )
        pieces.append(summed)
    rebuilt = sum_at_owner(jnp.concatenate(pieces, axis=1), FEAT, 0)
    offset = lax.axis_index(FEAT) * portion
    error_full = rebuilt + dec_row - lax.dynamic_slice_in_dim(target, offset, portion, 0)
    squared = over_axes(jnp.sum(error_full * error_full), SLOT_FEAT)
    error_half = collect(error_full.astype(jnp.bfloat16), FEAT, 0)
    mse = squared / (layers * tokens * D)
    dec_grads = []
    for a, b in pair_list:
        dec_grads.append(
            lax.dot_general(
                features[:, a * feature_dev : (a + 1) * feature_dev],
                error_half[:, b * width_dev : (b + 1) * width_dev],
                (((0,), (0,)), ((), ())),
                preferred_element_type=jnp.float32,
            )
        )
    row_block = error_half
    partials = []
    for upstream_a in range(layers):
        summed = jnp.zeros((tokens, feature_dev), jnp.float32)
        for b in range(upstream_a, layers):
            pair_num = pair_list.index((upstream_a, b))
            summed = summed + lax.dot_general(
                row_block[:, b * width_dev : (b + 1) * width_dev],
                dec_weight[pair_num],
                (((1,), (1,)), ((), ())),
                preferred_element_type=jnp.float32,
            )
        partials.append(summed)
    upstream = lax.psum(jnp.concatenate(partials, axis=1), SLOT)
    delta = upstream * slopes.astype(jnp.float32)
    bias_grad = jnp.sum(delta, axis=0).reshape(layers, feature_dev)
    delta_half = delta.astype(jnp.bfloat16)
    enc_grads = []
    for a in range(layers):
        enc_grads.append(
            lax.dot_general(
                acts_in[a],
                delta_half[:, a * feature_dev : (a + 1) * feature_dev],
                (((0,), (0,)), ((), ())),
                preferred_element_type=jnp.float32,
            )
        )
    return (jnp.stack(enc_grads), bias_grad, jnp.stack(dec_grads), mse)


def solution(mesh):
    split = Mesh(
        mesh.devices.reshape(2, 4, 2, 8, 2), ("slot_0", "slot_1", "feat_0", "feat_1", "feat_2")
    )
    in_specs = (
        P(None, None, SLOT),
        P(None, None, SLOT),
        P(None, SLOT, FEAT),
        P(None, FEAT),
        P(None, FEAT, SLOT),
        P(None, SLOT),
    )
    out_specs = (P(None, SLOT, FEAT), P(None, FEAT), P(None, FEAT, SLOT), P())
    return jax.shard_map(local, mesh=split, in_specs=in_specs, out_specs=out_specs, check_vma=False)
```

profile of v0, /device:TPU:32, one launch (start us, length us, event | category | flops | bytes accessed | tf_op | source)
XLA Modules:
  0.0 258.0 jit_solution(12020248933589295281)
XLA Ops:
  7.2 1.4 fusion.26
  8.6 1.4 fusion.28
  9.9 1.4 fusion.30
  11.3 1.3 pad_maximum_fusion.1
  12.6 87.5 %all-reduce.3.cloned.1.call-done = f32[256,1536]{1,0:T(8,128)} async-done(((f32[256,1536]{1,0:T(8,128)}), f32[256,1536]{1,0:T(8,128)}) %all-reduce.3.cloned.1.call-update) | async-done | bytes 1572880 | tf_op jit(solution)/shard_map/psum | solution.py:67
  100.1 1.6 maximum_convert_fusion
  101.7 0.3 fusion.14
  101.9 0.3 fusion.20
  102.2 0.3 fusion.24
  102.5 0.3 convolution_add_fusion.4
  102.8 0.3 convolution_add_fusion.3
  103.0 0.3 convolution_add_fusion.5
  103.3 0.1 pad_maximum_fusion.3
  103.4 1.2 copy.15
  104.6 9.8 %all-to-all-start = ((f32[32,8,864]{2,1,0:T(8,128)}), f32[32,8,864]{2,1,0:T(8,128)S(1)}, u32[]{:S(2)}, u32[]{:S(2)}) async-start(f32[32,8,864]{2,1,0:T(8,128)} %bitcast.107), calls=%async_computation | async-start | bytes 1835008 | tf_op jit(solution)/shard_map/all_to_all | solution.py:21
  114.5 2.0 convert_element_type.33
  116.5 2.0 constant_dynamic-slice_fusion
  118.5 1.2 copy.17
  119.6 0.1 add.67
  119.7 22.4 %all-to-all-done = f32[32,8,864]{2,1,0:T(8,128)S(1)} async-done(((f32[32,8,864]{2,1,0:T(8,128)}), f32[32,8,864]{2,1,0:T(8,128)S(1)}, u32[]{:S(2)}, u32[]{:S(2)}) %all-to-all-start) | async-done | bytes 884768 | tf_op jit(solution)/shard_map/all_to_all | solution.py:21
  142.1 0.1 reduce_sum.27
  142.2 0.6 multiply_reduce_fusion
  142.8 21.1 %all_to_all.10 = bf16[32,8,864]{2,1,0:T(8,128)(2,1)S(1)} all-to-all(bf16[32,8,864]{2,1,0:T(8,128)(2,1)S(1)} %broadcast_in_dim.12), channel_id=1, replica_groups=mesh['slot_0'=2,'slot_1'=4,'feat_0'=2,'feat_1'=8,'feat_2'=2] {'feat_0','..., dimensions={0} | all-to-all | bytes 884736 | tf_op jit(solution)/shard_map/all_to_all | solution.py:31
  163.9 0.3 fusion.22
  164.2 0.3 fusion.16
  164.6 0.3 fusion.8
  164.9 0.3 convolution_add_fusion.2
  165.3 0.3 convolution_add_fusion.1
  165.6 0.3 convolution_add_fusion
  166.0 1.3 pad_maximum_fusion.2
  167.3 5.6 %psum.51 = f32[]{:T(128)} all-reduce(f32[]{:T(128)} %get-tuple-element.6), channel_id=1, replica_groups=mesh['slot_0'=2,'slot_1'=4,'feat_0'=2,'feat_1'=8,'feat_2'=2] {'slot_0'}, use_global_device_ids=true, to_apply=%region_5.6 | all-reduce | flops 1 | bytes 8 | tf_op jit(solution)/shard_map/psum | solution.py:26
  172.8 9.6 %psum.52 = f32[]{:T(128)} all-reduce(f32[]{:T(128)} %psum.51), channel_id=1, replica_groups=mesh['slot_0'=2,'slot_1'=4,'feat_0'=2,'feat_1'=8,'feat_2'=2] {'slot_1'}, use_global_device_ids=true, to_apply=%region_6.7 | all-reduce | flops 1 | bytes 8 | tf_op jit(solution)/shard_map/psum | solution.py:26
  182.5 7.1 %psum.53 = f32[]{:T(128)} all-reduce(f32[]{:T(128)} %psum.52), channel_id=1, replica_groups=mesh['slot_0'=2,'slot_1'=4,'feat_0'=2,'feat_1'=8,'feat_2'=2] {'feat_0'}, use_global_device_ids=true, to_apply=%region_7.8 | all-reduce | flops 1 | bytes 8 | tf_op jit(solution)/shard_map/psum | solution.py:26
  189.5 15.8 %psum.54 = f32[]{:T(128)} all-reduce(f32[]{:T(128)} %psum.53), channel_id=1, replica_groups=mesh['slot_0'=2,'slot_1'=4,'feat_0'=2,'feat_1'=8,'feat_2'=2] {'feat_1'}, use_global_device_ids=true, to_apply=%region_8.9 | all-reduce | flops 1 | bytes 8 | tf_op jit(solution)/shard_map/psum | solution.py:26
  205.3 3.1 %psum.55 = f32[]{:T(128)} all-reduce(f32[]{:T(128)} %psum.54), channel_id=1, replica_groups=mesh['slot_0'=2,'slot_1'=4,'feat_0'=2,'feat_1'=8,'feat_2'=2] {'feat_2'}, use_global_device_ids=true, to_apply=%region_9.10 | all-reduce | flops 1 | bytes 8 | tf_op jit(solution)/shard_map/psum | solution.py:26
  209.0 1.1 fusion.5
  210.1 1.2 fusion.4
  211.3 1.2 fusion.3
  212.6 1.2 fusion.2
  213.8 1.2 fusion.1
  215.0 1.2 fusion
  216.2 29.3 %all-reduce.5.cloned.1.call-done = f32[256,1536]{1,0:T(8,128)} async-done(((f32[256,1536]{1,0:T(8,128)}), f32[256,1536]{1,0:T(8,128)}) %all-reduce.5.cloned.1.call-update) | async-done | bytes 1572880 | tf_op jit(solution)/shard_map/psum | solution.py:115
  245.5 1.8 fusion.6
  247.3 0.2 convolution_bitcast_fusion
  247.5 0.2 convolution_bitcast_fusion.1
  247.8 0.2 convolution_bitcast_fusion.2
  248.0 0.6 reshape.27
  248.6 1.3 pad_maximum_fusion
  (16 shorter events, 0.2 us)
Async XLA Ops:
  7.2 92.9 %all-reduce.3.cloned.1.call-start = ((), (), s32[]{:S(2)}) async-start(), calls=%async_computation.2 | async-start | bytes 3145728 | tf_op jit(solution)/shard_map/psum | solution.py:67
  11.3 1.3 copy-start.3
  12.6 89.1 %copy-start = (bf16[6,512,288]{1,2,0:T(8,128)(2,1)S(1)}, bf16[6,512,288]{1,2,0:T(8,128)(2,1)}, u32[]{:S(2)}) copy-start(bf16[6,512,288]{1,2,0:T(8,128)(2,1)} %param.10) | copy-start | bytes 5308420
  104.6 37.5 %all-to-all-start = ((f32[32,8,864]{2,1,0:T(8,128)}), f32[32,8,864]{2,1,0:T(8,128)S(1)}, u32[]{:S(2)}, u32[]{:S(2)}) async-start(f32[32,8,864]{2,1,0:T(8,128)} %bitcast.107), calls=%async_computation | async-start | bytes 1835008 | tf_op jit(solution)/shard_map/all_to_all | solution.py:21
  114.4 5.2 %copy-start.4 = (f32[3,288]{1,0:T(4,128)S(1)}, f32[3,288]{1,0:T(4,128)}, u32[]{:S(2)}) copy-start(f32[3,288]{1,0:T(4,128)} %param.11) | copy-start | bytes 10372
  114.4 131.1 %all-reduce.5.cloned.1.call-start = ((), (), s32[]{:S(2)}) async-start(), calls=%async_computation.3 | async-start | bytes 3145728 | tf_op jit(solution)/shard_map/psum | solution.py:115
  212.6 33.0 %copy-start.1 = (f32[256,1536]{1,0:T(8,128)S(1)}, f32[256,1536]{1,0:T(8,128)}, u32[]{:S(2)}) copy-start(f32[256,1536]{1,0:T(8,128)} %all-reduce.3.cloned.1.call-done) | copy-start | bytes 4718596
  216.2 31.1 %copy-start.2 = (bf16[3,256,288]{1,2,0:T(8,128)(2,1)S(1)}, bf16[3,256,288]{1,2,0:T(8,128)(2,1)}, u32[]{:S(2)}) copy-start(bf16[3,256,288]{1,2,0:T(8,128)(2,1)} %param.6) | copy-start | bytes 1327108
Sparse Core Ops, SparseCore 0:
  12.7 87.3 all-reduce.2
  167.4 78.1 all-reduce.4
where the time goes:
time: 259 us; the launch traced here: 258 us
  waiting for transfers between devices  139 us (54%)
  blocking collectives  62.2 us (24%)
  between operations  16 us (6%)
  matrix products  15.5 us (6%)
  other arithmetic  9.89 us (4%)
  starting transfers between devices  9.88 us (4%)
  local copies, waits for them, and re-layouts  5.13 us (2%)
    psum x1, waiting for transfers between devices, local(): preact = lax.psum(encode_rows(), SLOT) + bias_row  87.5 us
    psum x5, blocking collectives, over_axes(): return functools.reduce(lax.psum, axes, x)  41.1 us
    psum x1, waiting for transfers between devices, local(): upstream = lax.psum(jnp.concatenate(partials, axis=1), SLOT)  29.3 us
    all_to_all x1, waiting for transfers between devices, sum_at_owner(): lax.all_to_all(tiles, axis, split_axis=0, concat_axis=0, tiled=True)  22.4 us
    all_to_all x1, blocking collectives, sent_to_all(): lax.all_to_all(jnp.broadcast_to(x[None], (devices, *x.shape)), axis, 0, 0...  21.1 us
    all_to_all x1, starting transfers between devices, sum_at_owner(): lax.all_to_all(tiles, axis, split_axis=0, concat_axis=0, tiled=True)  9.8 us
    dot_general x6, matrix products, local(): lax.dot_general(features[:, a * feature_dev:(a + 1) * feature_dev], error...  7.18 us
  transfers between devices with their start and end apart: 3, of which 3 were waited for; matrix products, arithmetic and copies ran while one was open for 5% of the time, Pallas kernels for 0%

commit v1 on v0

--- a/solution.py
+++ b/solution.py
@@ -64,7 +64,7 @@
         return jnp.concatenate(pieces, axis=1)
 
     bias_row = enc_bias.reshape(1, layers * feature_dev)
-    preact = lax.psum(encode_rows(), SLOT) + bias_row
+    preact = lax.psum(lax.psum(encode_rows(), "slot_1"), "slot_0") + bias_row
     features, slopes = activate(preact)
     target = (
         jnp.transpose(acts_out, (1, 0, 2)).reshape(tokens, layers * width_dev).astype(jnp.float32)

time: 259 us -> 296 us (1.14)
  waiting for transfers between devices: 139 us -> 176 us
    psum x1 -> x2, waiting for transfers between devices: 87.5 us -> 124 us  [local(): preact = lax.psum(lax.psum(encode_rows(), 'slot_1'), 'slot_0') + bias_row]
  transfers between devices with their start and end apart: 3 -> 4, of which waited for: 3 -> 4; matrix products, arithmetic and copies ran while one was open for 5% -> 4% of each run, Pallas kernels for 0% -> 0%
where the time goes in v1:
time: 296 us
  waiting for transfers between devices  176 us (59%)
  blocking collectives  63.9 us (22%)
  between operations  15.7 us (5%)
  matrix products  15.5 us (5%)
  starting transfers between devices  9.91 us (3%)
  other arithmetic  9.89 us (3%)
  local copies, waits for them, and re-layouts  5.12 us (2%)
    psum x2, waiting for transfers between devices, local(): preact = lax.psum(lax.psum(encode_rows(), 'slot_1'), 'slot_0') + bias_row  124 us
    psum x5, blocking collectives, over_axes(): return functools.reduce(lax.psum, axes, x)  42.8 us
    psum x1, waiting for transfers between devices, local(): upstream = lax.psum(jnp.concatenate(partials, axis=1), SLOT)  29.1 us
    all_to_all x1, waiting for transfers between devices, sum_at_owner(): lax.all_to_all(tiles, axis, split_axis=0, concat_axis=0, tiled=True)  22.4 us
    all_to_all x1, blocking collectives, sent_to_all(): lax.all_to_all(jnp.broadcast_to(x[None], (devices, *x.shape)), axis, 0, 0...  21.1 us
    all_to_all x1, starting transfers between devices, sum_at_owner(): lax.all_to_all(tiles, axis, split_axis=0, concat_axis=0, tiled=True)  9.78 us
    dot_general x6, matrix products, local(): lax.dot_general(features[:, a * feature_dev:(a + 1) * feature_dev], error...  7.18 us
  transfers between devices with their start and end apart: 4, of which 4 were waited for; matrix products, arithmetic and copies ran while one was open for 4% of the time, Pallas kernels for 0%

profile of v1, /device:TPU:32, one launch (start us, length us, event | category | flops | bytes accessed | tf_op | source)
XLA Modules:
  0.0 295.8 jit_solution(13100654409273868253)
XLA Ops:
  7.2 1.4 fusion.26
  8.6 1.4 fusion.28
  9.9 1.4 fusion.30
  11.3 1.3 pad_maximum_fusion.1
  12.6 58.3 %all-reduce.4.cloned.1.call-done = f32[256,1536]{1,0:T(8,128)} async-done(((f32[256,1536]{1,0:T(8,128)}), f32[256,1536]{1,0:T(8,128)}) %all-reduce.4.cloned.1.call-update) | async-done | bytes 1572880 | tf_op jit(solution)/shard_map/psum | solution.py:67
  71.0 65.9 %all-reduce.6.cloned.1.call-done = f32[256,1536]{1,0:T(8,128)} async-done(((f32[256,1536]{1,0:T(8,128)}), f32[256,1536]{1,0:T(8,128)}) %all-reduce.6.cloned.1.call-update) | async-done | bytes 1572880 | tf_op jit(solution)/shard_map/psum | solution.py:67
  136.9 1.6 maximum_convert_fusion
  138.5 0.3 fusion.14
  138.7 0.3 fusion.20
  139.0 0.3 fusion.24
  139.3 0.3 convolution_add_fusion.4
  139.5 0.3 convolution_add_fusion.3
  139.8 0.3 convolution_add_fusion.5
  140.2 1.2 copy.15
  141.4 9.8 %all-to-all-start = ((f32[32,8,864]{2,1,0:T(8,128)}), f32[32,8,864]{2,1,0:T(8,128)S(1)}, u32[]{:S(2)}, u32[]{:S(2)}) async-start(f32[32,8,864]{2,1,0:T(8,128)} %bitcast.107), calls=%async_computation | async-start | bytes 1835008 | tf_op jit(solution)/shard_map/all_to_all | solution.py:21
  151.3 2.0 convert_element_type.33
  153.3 2.0 constant_dynamic-slice_fusion
  155.2 1.2 copy.17
  156.4 0.1 add.69
  156.5 22.4 %all-to-all-done = f32[32,8,864]{2,1,0:T(8,128)S(1)} async-done(((f32[32,8,864]{2,1,0:T(8,128)}), f32[32,8,864]{2,1,0:T(8,128)S(1)}, u32[]{:S(2)}, u32[]{:S(2)}) %all-to-all-start) | async-done | bytes 884768 | tf_op jit(solution)/shard_map/all_to_all | solution.py:21
  178.9 0.1 reduce_sum.27
  178.9 0.6 multiply_reduce_fusion
  179.6 21.1 %all_to_all.10 = bf16[32,8,864]{2,1,0:T(8,128)(2,1)S(1)} all-to-all(bf16[32,8,864]{2,1,0:T(8,128)(2,1)S(1)} %broadcast_in_dim.12), channel_id=1, replica_groups=mesh['slot_0'=2,'slot_1'=4,'feat_0'=2,'feat_1'=8,'feat_2'=2] {'feat_0','..., dimensions={0} | all-to-all | bytes 884736 | tf_op jit(solution)/shard_map/all_to_all | solution.py:31
  200.7 0.3 fusion.22
  201.0 0.3 fusion.16
  201.3 0.3 fusion.8
  201.7 0.3 convolution_add_fusion.2
  202.0 0.3 convolution_add_fusion.1
  202.4 0.3 convolution_add_fusion
  202.7 1.3 pad_maximum_fusion.2
  204.0 5.6 %psum.59 = f32[]{:T(128)} all-reduce(f32[]{:T(128)} %get-tuple-element.6), channel_id=1, replica_groups=mesh['slot_0'=2,'slot_1'=4,'feat_0'=2,'feat_1'=8,'feat_2'=2] {'slot_0'}, use_global_device_ids=true, to_apply=%region_6.7 | all-reduce | flops 1 | bytes 8 | tf_op jit(solution)/shard_map/psum | solution.py:26
  209.6 11.0 %psum.60 = f32[]{:T(128)} all-reduce(f32[]{:T(128)} %psum.59), channel_id=1, replica_groups=mesh['slot_0'=2,'slot_1'=4,'feat_0'=2,'feat_1'=8,'feat_2'=2] {'slot_1'}, use_global_device_ids=true, to_apply=%region_7.8 | all-reduce | flops 1 | bytes 8 | tf_op jit(solution)/shard_map/psum | solution.py:26
  220.6 7.1 %psum.61 = f32[]{:T(128)} all-reduce(f32[]{:T(128)} %psum.60), channel_id=1, replica_groups=mesh['slot_0'=2,'slot_1'=4,'feat_0'=2,'feat_1'=8,'feat_2'=2] {'feat_0'}, use_global_device_ids=true, to_apply=%region_8.9 | all-reduce | flops 1 | bytes 8 | tf_op jit(solution)/shard_map/psum | solution.py:26
  227.7 16.0 %psum.62 = f32[]{:T(128)} all-reduce(f32[]{:T(128)} %psum.61), channel_id=1, replica_groups=mesh['slot_0'=2,'slot_1'=4,'feat_0'=2,'feat_1'=8,'feat_2'=2] {'feat_1'}, use_global_device_ids=true, to_apply=%region_9.10 | all-reduce | flops 1 | bytes 8 | tf_op jit(solution)/shard_map/psum | solution.py:26
  243.7 3.1 %psum.63 = f32[]{:T(128)} all-reduce(f32[]{:T(128)} %psum.62), channel_id=1, replica_groups=mesh['slot_0'=2,'slot_1'=4,'feat_0'=2,'feat_1'=8,'feat_2'=2] {'feat_2'}, use_global_device_ids=true, to_apply=%region_10.11 | all-reduce | flops 1 | bytes 8 | tf_op jit(solution)/shard_map/psum | solution.py:26
  247.4 1.1 fusion.5
  248.5 1.2 fusion.4
  249.8 1.2 fusion.3
  251.0 1.2 fusion.2
  252.2 1.2 fusion.1
  253.4 1.2 fusion
  254.6 29.1 %all-reduce.8.cloned.1.call-done = f32[256,1536]{1,0:T(8,128)} async-done(((f32[256,1536]{1,0:T(8,128)}), f32[256,1536]{1,0:T(8,128)}) %all-reduce.8.cloned.1.call-update) | async-done | bytes 1572880 | tf_op jit(solution)/shard_map/psum | solution.py:115
  283.7 1.8 fusion.6
  285.5 0.2 convolution_bitcast_fusion
  285.7 0.2 convolution_bitcast_fusion.1
  286.0 0.2 convolution_bitcast_fusion.2
  286.2 0.6 reshape.27
  286.8 1.3 pad_maximum_fusion
  (19 shorter events, 0.3 us)
Async XLA Ops:
  7.2 63.8 %all-reduce.4.cloned.1.call-start = ((), (), s32[]{:S(2)}) async-start(), calls=%async_computation.2 | async-start | bytes 3145728 | tf_op jit(solution)/shard_map/psum | solution.py:67
  12.6 58.4 %copy-start.3 = (f32[3,512]{1,0:T(4,128)S(1)}, f32[3,512]{1,0:T(4,128)}, u32[]{:S(2)}) copy-start(f32[3,512]{1,0:T(4,128)} %param.9) | copy-start | bytes 18436
  12.6 124.3 %all-reduce.6.cloned.1.call-start = ((), (), s32[]{:S(2)}) async-start(), calls=%async_computation.3 | async-start | bytes 3145728 | tf_op jit(solution)/shard_map/psum | solution.py:67
  70.9 67.5 %copy-start = (bf16[6,512,288]{1,2,0:T(8,128)(2,1)S(1)}, bf16[6,512,288]{1,2,0:T(8,128)(2,1)}, u32[]{:S(2)}) copy-start(bf16[6,512,288]{1,2,0:T(8,128)(2,1)} %param.10) | copy-start | bytes 5308420
  141.4 37.5 %all-to-all-start = ((f32[32,8,864]{2,1,0:T(8,128)}), f32[32,8,864]{2,1,0:T(8,128)S(1)}, u32[]{:S(2)}, u32[]{:S(2)}) async-start(f32[32,8,864]{2,1,0:T(8,128)} %bitcast.107), calls=%async_computation | async-start | bytes 1835008 | tf_op jit(solution)/shard_map/all_to_all | solution.py:21
  151.2 5.2 %copy-start.4 = (f32[3,288]{1,0:T(4,128)S(1)}, f32[3,288]{1,0:T(4,128)}, u32[]{:S(2)}) copy-start(f32[3,288]{1,0:T(4,128)} %param.11) | copy-start | bytes 10372
  151.2 132.5 %all-reduce.8.cloned.1.call-start = ((), (), s32[]{:S(2)}) async-start(), calls=%async_computation.4 | async-start | bytes 3145728 | tf_op jit(solution)/shard_map/psum | solution.py:115
  251.0 32.7 %copy-start.1 = (f32[256,1536]{1,0:T(8,128)S(1)}, f32[256,1536]{1,0:T(8,128)}, u32[]{:S(2)}) copy-start(f32[256,1536]{1,0:T(8,128)} %all-reduce.6.cloned.1.call-done) | copy-start | bytes 4718596
  254.6 30.8 %copy-start.2 = (bf16[3,256,288]{1,2,0:T(8,128)(2,1)S(1)}, bf16[3,256,288]{1,2,0:T(8,128)(2,1)}, u32[]{:S(2)}) copy-start(bf16[3,256,288]{1,2,0:T(8,128)(2,1)} %param.6) | copy-start | bytes 1327108
Sparse Core Ops, SparseCore 0:
  12.7 58.1 all-reduce.3
  73.5 63.3 all-reduce.5
  204.1 79.5 all-reduce.7
